TPU v7x, 32 devices: a whole 2x2x4 slice. The times are simulated.
32 devices in a mesh: groups: 2 (over y), gx: 4 (over z), gy: 2 (over x), gz: 2 (over core).
Axes of the slice: x: 2, y: 2, z: 4, core: 2. Of those that a mesh axis runs over, the one named last changes fastest.
Arguments:
- features: bfloat16 [32, 8, 32, 128], P(('groups', 'gx'), 'gy', 'gz'), parts along dimension 0, may hold values from -6 to 6
- scales: bfloat16 [32, 8, 32, 128], P(('groups', 'gx'), 'gy', 'gz'), parts along dimension 0, may hold values from 0.29882812 to 3
- occupancy: int32 [8, 2, 8], P(('groups', 'gx'), 'gy', 'gz'), parts along dimension 0, may hold values 0 or 1
- kernel: bfloat16 [62, 128, 128], replicated, may hold values from -0.0625 to 0.0625
- gamma: float32 [128, 128], replicated, may hold values from 0 to 0.015625
- beta: float32 [128], replicated, may hold values from 0.5 to 2
Outputs:
- grad_features: bfloat16 [32, 8, 32, 128], P(('groups', 'gx'), 'gy', 'gz'), parts along dimension 0
- grad_kernel: float32 [2031616], P(('groups', 'gx', 'gy', 'gz')), parts along dimension 0
- grad_gamma: float32 [256, 128], P('groups'), parts along dimension 0
- grad_beta: float32 [256], P('groups'), parts along dimension 0
There are 2 independent parts, one for each index of `groups`. A program takes and returns all parts, laid end to end along the dimension named above; an argument that names none is the same for every part. Nothing has to cross between parts.
All inputs are finite; a program needn't handle non-finite values. No bound on the sum of `occupancy` on one device may be relied on, other than what follows from the above.
Results may differ from a plain program's by a relative error of at most 0.0039.
The roundings to bfloat16 on the way count: a program that leaves them out, or rounds other values in their place, can miss the bound.
Values may be sent and summed in bfloat16 or wider, within the bound.
No kernel may reach another device: no remote copies, remote signals or barrier semaphores. Data moves between devices by JAX's collectives and lax.ppermute only.
A program may use at most 64 MiB of HBM per device.

v0:
```python
import math
import jax
import jax.numpy as jnp
from jax import lax
from jax.sharding import PartitionSpec as P

OB = 4


def padded_2(shard, sides, width):
    for axis, dim in sides:
        size, length = (lax.axis_size(axis), shard.shape[dim])
        up = [(i, (i + 1) % size) for i in range(size - 1)]
        down = [(j, i) for i, j in up]
        last = lax.slice_in_dim(shard, length - width, length, axis=dim)
        leading = lax.slice_in_dim(shard, 0, width, axis=dim)
        before = lax.ppermute(last, axis, up)
        after = lax.ppermute(leading, axis, down)
        shard = jnp.concatenate([before, shard, after], axis=dim)
    return shard


def from_behind(value, axis, steps):
    count = lax.axis_size(axis)
    leading, last = (max(0, -steps), min(count, count - steps))
    return lax.ppermute(value, axis, [(source, source + steps) for source in range(leading, last)])


def causal_offsets():
    result = []
    for along_x in range(-2, 3):
        for along_y in range(-2, 3):
            for along_z in range(-2, 3):
                if (along_x, along_y, along_z) < (0, 0, 0):
                    result.append((along_x, along_y, along_z))
    return result


def tap_groups():
    groups = []
    for number, offset in enumerate(causal_offsets()):
        if groups and groups[-1][0] == offset[0] and (groups[-1][1] == offset[1]):
            groups[-1][3] += 1
        else:
            groups.append([offset[0], offset[1], offset[2], 1, number])
    return groups


def expand_blocks(occupancy, edge):
    blocks_x, blocks_y, blocks_z = occupancy.shape
    grown = jnp.broadcast_to(
        occupancy[:, None, :, None, :, None], (blocks_x, edge, blocks_y, edge, blocks_z, edge)
    )
    return grown.reshape(-1, 1).astype(jnp.float32)


def forward_patch(padded, along_x, along_y, start_z, count, extent):
    size_x, size_y, size_z = extent
    pieces = [
        padded[
            2 + along_x : 2 + along_x + size_x,
            2 + along_y : 2 + along_y + size_y,
            2 + along_z : 2 + along_z + size_z,
        ]
        for along_z in range(start_z, start_z + count)
    ]
    return jnp.concatenate(pieces, axis=3).reshape(size_x * size_y * size_z, -1)


def context_mean(padded, kernel, extent):
    channels = kernel.shape[1]
    total = jnp.zeros((extent[0] * extent[1] * extent[2], channels), jnp.float32)
    for along_x, along_y, start_z, count, first_tap in tap_groups():
        patch = forward_patch(padded, along_x, along_y, start_z, count, extent)
        weights = kernel[first_tap : first_tap + count].reshape(count * channels, channels)
        total = total + jnp.dot(patch, weights, preferred_element_type=jnp.float32)
    return total


def context_transposed(padded, kernel, extent):
    size_x, size_y, size_z = extent
    channels = kernel.shape[1]
    total = jnp.zeros((size_x * size_y * size_z, channels), jnp.float32)
    for along_x, along_y, start_z, count, first_tap in tap_groups():
        pieces = [
            padded[
                -along_x : -along_x + size_x,
                2 - along_y : 2 - along_y + size_y,
                2 - along_z : 2 - along_z + size_z,
            ]
            for along_z in range(start_z, start_z + count)
        ]
        patch = jnp.concatenate(pieces, axis=3).reshape(size_x * size_y * size_z, -1)
        weights = jnp.transpose(kernel[first_tap : first_tap + count], (0, 2, 1)).reshape(
            count * channels, channels
        )
        total = total + jnp.dot(patch, weights, preferred_element_type=jnp.float32)
    return total


def kernel_terms(padded, mean_grad, extent):
    terms = []
    for along_x, along_y, start_z, count, first_tap in tap_groups():
        patch = forward_patch(padded, along_x, along_y, start_z, count, extent)
        terms.append(
            lax.dot_general(
                patch, mean_grad, (((0,), (0,)), ((), ())), preferred_element_type=jnp.float32
            )
        )
    return jnp.concatenate(terms, axis=0).reshape(-1)


def lower_sides_first(latent):
    widened = padded_2(latent, (("gy", 1), ("gz", 2)), 2)
    below = from_behind(widened[-2:], "gx", 1)
    return jnp.concatenate([below, widened], axis=0)


def upper_sides_first(grads):
    widened = padded_2(grads, (("gy", 1), ("gz", 2)), 2)
    above = from_behind(widened[:2], "gx", -1)
    return jnp.concatenate([widened, above], axis=0)


def local(features, scales, occupancy, kernel, gamma, beta):
    size_x, size_y, size_z, channels = features.shape
    extent = (size_x, size_y, size_z)
    voxels = size_x * size_y * size_z
    feats = features.astype(jnp.float32).reshape(voxels, channels)
    occupied = expand_blocks(occupancy, OB)
    energy = beta[None, :] + jnp.dot(
        feats * feats, gamma, precision=lax.Precision.HIGHEST, preferred_element_type=jnp.float32
    )
    inv_root = lax.rsqrt(energy)
    latent = (occupied * feats * inv_root).astype(jnp.bfloat16)
    latent_grid = latent.reshape(size_x, size_y, size_z, channels)
    padded = lower_sides_first(latent_grid)
    mean = context_mean(padded, kernel, extent)
    latent_f = latent.astype(jnp.float32)
    scale_f = scales.astype(jnp.float32).reshape(voxels, channels)
    inverse = 1.0 / (scale_f * scale_f)
    mean_grad = (occupied * (mean - latent_f) * inverse).astype(jnp.bfloat16)
    grad_grid = mean_grad.reshape(size_x, size_y, size_z, channels)
    grad_pad = upper_sides_first(grad_grid)
    context_grad = context_transposed(grad_pad, kernel, extent)
    latent_grad = occupied * (context_grad + (latent_f - mean) * inverse)
    weighted = latent_grad * feats * inv_root * inv_root * inv_root
    coupled = jnp.dot(
        weighted, gamma.T, precision=lax.Precision.HIGHEST, preferred_element_type=jnp.float32
    )
    grad_features = (
        (latent_grad * inv_root - feats * coupled)
        .astype(jnp.bfloat16)
        .reshape(size_x, size_y, size_z, channels)
    )
    kernel_local = kernel_terms(padded, mean_grad, extent) / voxels
    grad_kernel = lax.psum_scatter(
        kernel_local, ("gx", "gy", "gz"), scatter_dimension=0, tiled=True
    )
    factor = 0.5 / math.sqrt(voxels)
    gamma_local = -factor * jnp.dot(
        (feats * feats).T,
        weighted,
        precision=lax.Precision.HIGHEST,
        preferred_element_type=jnp.float32,
    )
    beta_local = -factor * jnp.sum(weighted, axis=0)
    grad_gamma, grad_beta = lax.psum((gamma_local, beta_local), ("gx", "gy", "gz"))
    return (grad_features, grad_kernel, grad_gamma, grad_beta)


def solution(mesh):
    return jax.shard_map(
        local,
        mesh=mesh,
        in_specs=(
            P(("groups", "gx"), "gy", "gz", None),
            P(("groups", "gx"), "gy", "gz", None),
            P(("groups", "gx"), "gy", "gz"),
            P(),
            P(),
            P(),
        ),
        out_specs=(
            P(("groups", "gx"), "gy", "gz", None),
            P(("groups", "gx", "gy", "gz")),
            P("groups", None),
            P("groups"),
        ),
        check_vma=False,
    )
```

profile of v0, /device:TPU:0, one launch (start us, length us, event | category | flops | bytes accessed | tf_op | source)
XLA Modules:
  0.0 195.3 jit_solution(11821745433101948663)
XLA Ops:
  8.1 1.2 fusion.12
  9.3 4.9 %collective-permute-start = (bf16[4,2,16,128]{3,2,1,0:T(8,128)(2,1)S(1)}, bf16[4,2,16,128]{3,2,1,0:T(8,128)(2,1)S(1)}, u32[]{:S(2)}, u32[]{:S(2)}) collective-permute-start(bf16[4,2,16,128]{3,2,1,0:T(8,128)(2,1)S(1)} %get-tuple-element.160), channel_id=1, source_target_pairs={{0,2},{1,3},{4,6},{5,7},{8,10},{9,11},{12,14},{13,15},{16,18},{17,... | collective-permute-start | bytes 98312 | tf_op jit(solution)/shard_map/ppermute | solution.py:17
  14.2 1.3 collective-permute-start.1
  15.5 2.1 %fusion.16 = (bf16[5,128,128]{2,1,0:T(8,128)(2,1)}, bf16[5,128,128]{2,1,0:T(8,128)(2,1)}, bf16[5,128,128]{2,1,0:T(8,128)(2,1)}, bf16[5,128,128]{2,1,0:T(8,128)(2,1)}, bf16[5,128,128]{2,1,0:T(8,128)(2,1)}) fusion(bf16[62,128,128]{2,1,0:T(8,128)(2,1)} %param.9), kind=kLoop, calls=%fused_computation.225 | loop fusion | bytes 1638400 | tf_op jit(solution)/shard_map/slice | solution.py:75
  17.7 3.0 %slice_bitcast_fusion.1 = (bf16[5,128,128]{1,2,0:T(8,128)(2,1)S(1)}, bf16[5,128,128]{1,2,0:T(8,128)(2,1)S(1)}, bf16[5,128,128]{1,2,0:T(8,128)(2,1)S(1)}, bf16[5,...) fusion(bf16[62,128,128]{2,1,0:T(8,128)(2,1)} %param.9), kind=kLoop, calls=%fused_computation.212 | loop fusion | bytes 5079040 | tf_op jit(solution)/shard_map/transpose | solution.py:94
  20.6 0.9 slice_bitcast_fusion
  22.2 1.3 collective-permute-start.3
  23.5 3.6 %collective-permute-start.2 = (bf16[4,8,2,128]{3,2,1,0:T(2,128)(2,1)}, bf16[4,8,2,128]{3,2,1,0:T(2,128)(2,1)}, u32[]{:S(2)}, u32[]{:S(2)}) collective-permute-start(bf16[4,8,2,128]{3,2,1,0:T(2,128)(2,1)} %get-tuple-element.153), channel_id=1, source_target_pairs={{0,1},{2,3},{4,5},{6,7},{8,9},{10,11},{12,13},{14,15},{16,17},{18,... | collective-permute-start | bytes 49160 | tf_op jit(solution)/shard_map/ppermute | solution.py:17
  34.0 3.5 %collective-permute-start.4 = (bf16[2,8,20,128]{3,2,1,0:T(8,128)(2,1)S(1)}, bf16[2,8,20,128]{3,2,1,0:T(8,128)(2,1)S(1)}, u32[]{:S(2)}, u32[]{:S(2)}) collective-permute-start(bf16[2,8,20,128]{3,2,1,0:T(8,128)(2,1)S(1)} %pad_maximum_fusion.9), channel_id=1, source_target_pairs={{0,4},{4,8},{8,12},{1,5},{5,9},{9,13},{2,6},{6,10},{10,14},{3,7},{... | collective-permute-start | bytes 245768 | tf_op jit(solution)/shard_map/ppermute | solution.py:26
  38.8 0.9 collective-permute-done.4
  44.9 4.5 %collective-permute-start.5 = (bf16[4,2,16,128]{3,2,1,0:T(8,128)(2,1)S(1)}, bf16[4,2,16,128]{3,2,1,0:T(8,128)(2,1)S(1)}, u32[]{:S(2)}, u32[]{:S(2)}) collective-permute-start(bf16[4,2,16,128]{3,2,1,0:T(8,128)(2,1)S(1)} %get-tuple-element.158), channel_id=1, source_target_pairs={{0,2},{1,3},{4,6},{5,7},{8,10},{9,11},{12,14},{13,15},{16,18},{17,... | collective-permute-start | bytes 98312 | tf_op jit(solution)/shard_map/ppermute | solution.py:17
  49.4 1.3 collective-permute-start.6
  54.3 0.9 collective-permute-done.6
  55.3 1.3 collective-permute-start.7
  56.6 1.4 collective-permute-start.8
  58.0 2.2 %multiply_bitcast_fusion = f32[1015808]{0:T(1024)} fusion(f32[7936,128]{1,0:T(8,128)S(1)} %convolution_dynamic-update-slice_fusion.12), kind=kLoop, calls=%fused_computation | loop fusion | flops 1015808 | bytes 8126464 | tf_op jit(solution)/shard_map/div | solution.py:156
  60.3 1.5 collective-permute-start.9
  62.4 5.4 %collective-permute-done.9 = bf16[2,8,20,128]{3,2,1,0:T(8,128)(2,1)S(1)} collective-permute-done((bf16[2,8,20,128]{3,2,1,0:T(8,128)(2,1)S(1)}, bf16[2,8,20,128]{3,2,1,0:T(8,128)(2,1)S(1)}, u32[]{:S(2)}, u32[]{:S(2)}) %collective-permute-start.9) | collective-permute-done | bytes 81952 | tf_op jit(solution)/shard_map/ppermute | solution.py:26
  72.1 1.0 convolution_multiply_fusion.1
  74.4 34.5 %psum.15 = f32[128]{0:T(128)} all-reduce(f32[128]{0:T(128)S(1)} %broadcast_multiply_fusion), channel_id=1, replica_groups=mesh['groups'=2,'gx'=4,'gy'=2,'gz'=2] {'gx','gy','gz'}, use_global_device_ids=true, to_apply=%region_3.0 | all-reduce | flops 128 | bytes 1024 | tf_op jit(solution)/shard_map/psum | solution.py:168
  108.9 0.9 fusion.6
  109.8 75.5 %all-reduce.4.cloned.1.call-done = (f32[1015808]{0:T(1024)}, f32[128,128]{1,0:T(8,128)}) async-done(((f32[1015808]{0:T(1024)}, f32[128,128]{1,0:T(8,128)}), (f32[1015808]{0:T(1024)}, f32[128,128]{1,0:T(8,128)})) %all-reduce.4.cloned.1.call-update) | async-done | bytes 4128784
  185.3 1.7 dynamic-slice.1
  186.9 1.5 copy.159
  (143 shorter events, 23.4 us)
Async XLA Ops:
  7.2 178.1 %all-reduce.4.cloned.1.call-start = ((), (), s32[]{:S(2)}) async-start(), calls=%async_computation | async-start | bytes 8257536
  8.1 19.0 %copy-start.14 = (bf16[4,4,16,128]{3,2,1,0:T(8,128)(2,1)S(1)}, bf16[4,4,16,128]{3,2,1,0:T(8,128)(2,1)}, u32[]{:S(2)}) copy-start(bf16[4,4,16,128]{3,2,1,0:T(8,128)(2,1)} %param.7) | copy-start | bytes 196612
  9.3 12.2 %collective-permute-start = (bf16[4,2,16,128]{3,2,1,0:T(8,128)(2,1)S(1)}, bf16[4,2,16,128]{3,2,1,0:T(8,128)(2,1)S(1)}, u32[]{:S(2)}, u32[]{:S(2)}) collective-permute-start(bf16[4,2,16,128]{3,2,1,0:T(8,128)(2,1)S(1)} %get-tuple-element.160), channel_id=1, source_target_pairs={{0,2},{1,3},{4,6},{5,7},{8,10},{9,11},{12,14},{13,15},{16,18},{17,... | collective-permute-start | bytes 98312 | tf_op jit(solution)/shard_map/ppermute | solution.py:17
  14.2 7.3 %collective-permute-start.1 = (bf16[4,2,16,128]{3,2,1,0:T(8,128)(2,1)S(1)}, bf16[4,2,16,128]{3,2,1,0:T(8,128)(2,1)S(1)}, u32[]{:S(2)}, u32[]{:S(2)}) collective-permute-start(bf16[4,2,16,128]{3,2,1,0:T(8,128)(2,1)S(1)} %get-tuple-element.161), channel_id=1, source_target_pairs={{2,0},{3,1},{6,4},{7,5},{10,8},{11,9},{14,12},{15,13},{18,16},{19,... | collective-permute-start | bytes 98312 | tf_op jit(solution)/shard_map/ppermute | solution.py:18
  22.2 11.1 %collective-permute-start.3 = (bf16[4,8,2,128]{3,2,1,0:T(2,128)(2,1)}, bf16[4,8,2,128]{3,2,1,0:T(2,128)(2,1)S(1)}, u32[]{:S(2)}, u32[]{:S(2)}) collective-permute-start(bf16[4,8,2,128]{3,2,1,0:T(2,128)(2,1)} %get-tuple-element.152), channel_id=1, source_target_pairs={{1,0},{3,2},{5,4},{7,6},{9,8},{11,10},{13,12},{15,14},{17,16},{19,... | collective-permute-start | bytes 49160 | tf_op jit(solution)/shard_map/ppermute | solution.py:18
  23.5 9.8 %collective-permute-start.2 = (bf16[4,8,2,128]{3,2,1,0:T(2,128)(2,1)}, bf16[4,8,2,128]{3,2,1,0:T(2,128)(2,1)}, u32[]{:S(2)}, u32[]{:S(2)}) collective-permute-start(bf16[4,8,2,128]{3,2,1,0:T(2,128)(2,1)} %get-tuple-element.153), channel_id=1, source_target_pairs={{0,1},{2,3},{4,5},{6,7},{8,9},{10,11},{12,13},{14,15},{16,17},{18,... | collective-permute-start | bytes 49160 | tf_op jit(solution)/shard_map/ppermute | solution.py:17
  34.0 5.7 %collective-permute-start.4 = (bf16[2,8,20,128]{3,2,1,0:T(8,128)(2,1)S(1)}, bf16[2,8,20,128]{3,2,1,0:T(8,128)(2,1)S(1)}, u32[]{:S(2)}, u32[]{:S(2)}) collective-permute-start(bf16[2,8,20,128]{3,2,1,0:T(8,128)(2,1)S(1)} %pad_maximum_fusion.9), channel_id=1, source_target_pairs={{0,4},{4,8},{8,12},{1,5},{5,9},{9,13},{2,6},{6,10},{10,14},{3,7},{... | collective-permute-start | bytes 245768 | tf_op jit(solution)/shard_map/ppermute | solution.py:26
  38.4 3.2 %copy-start.7 = (bf16[5,128,128]{2,1,0:T(8,128)(2,1)S(1)}, bf16[5,128,128]{2,1,0:T(8,128)(2,1)}, u32[]{:S(2)}) copy-start(bf16[5,128,128]{2,1,0:T(8,128)(2,1)} %get-tuple-element.33) | copy-start | bytes 491524
  38.7 3.2 %copy-start.6 = (bf16[5,128,128]{2,1,0:T(8,128)(2,1)S(1)}, bf16[5,128,128]{2,1,0:T(8,128)(2,1)}, u32[]{:S(2)}) copy-start(bf16[5,128,128]{2,1,0:T(8,128)(2,1)} %get-tuple-element.32) | copy-start | bytes 491524
  40.6 1.8 copy-start.4
  40.6 2.0 %copy-start.2 = (bf16[5,128,128]{2,1,0:T(8,128)(2,1)S(1)}, bf16[5,128,128]{2,1,0:T(8,128)(2,1)}, u32[]{:S(2)}) copy-start(bf16[5,128,128]{2,1,0:T(8,128)(2,1)} %get-tuple-element.26) | copy-start | bytes 491524
  41.6 2.7 %copy-start.12 = (bf16[5,128,128]{2,1,0:T(8,128)(2,1)S(1)}, bf16[5,128,128]{2,1,0:T(8,128)(2,1)}, u32[]{:S(2)}) copy-start(bf16[5,128,128]{2,1,0:T(8,128)(2,1)} %get-tuple-element.29) | copy-start | bytes 491524
  41.6 2.7 %copy-start.16 = (f32[256]{0:T(256)S(1)}, f32[256]{0:T(256)}, u32[]{:S(2)}) copy-start(f32[256]{0:T(256)} %copy-done.15) | copy-start | bytes 3076
  44.9 9.4 %collective-permute-start.5 = (bf16[4,2,16,128]{3,2,1,0:T(8,128)(2,1)S(1)}, bf16[4,2,16,128]{3,2,1,0:T(8,128)(2,1)S(1)}, u32[]{:S(2)}, u32[]{:S(2)}) collective-permute-start(bf16[4,2,16,128]{3,2,1,0:T(8,128)(2,1)S(1)} %get-tuple-element.158), channel_id=1, source_target_pairs={{0,2},{1,3},{4,6},{5,7},{8,10},{9,11},{12,14},{13,15},{16,18},{17,... | collective-permute-start | bytes 98312 | tf_op jit(solution)/shard_map/ppermute | solution.py:17
  49.4 5.8 %collective-permute-start.6 = (bf16[4,2,16,128]{3,2,1,0:T(8,128)(2,1)S(1)}, bf16[4,2,16,128]{3,2,1,0:T(8,128)(2,1)S(1)}, u32[]{:S(2)}, u32[]{:S(2)}) collective-permute-start(bf16[4,2,16,128]{3,2,1,0:T(8,128)(2,1)S(1)} %get-tuple-element.159), channel_id=1, source_target_pairs={{2,0},{3,1},{6,4},{7,5},{10,8},{11,9},{14,12},{15,13},{18,16},{19,... | collective-permute-start | bytes 98312 | tf_op jit(solution)/shard_map/ppermute | solution.py:18
  55.3 4.9 %collective-permute-start.7 = (bf16[4,8,2,128]{3,2,1,0:T(2,128)(2,1)S(1)}, bf16[4,8,2,128]{3,2,1,0:T(2,128)(2,1)S(1)}, u32[]{:S(2)}, u32[]{:S(2)}) collective-permute-start(bf16[4,8,2,128]{3,2,1,0:T(2,128)(2,1)S(1)} %get-tuple-element.148), channel_id=1, source_target_pairs={{0,1},{2,3},{4,5},{6,7},{8,9},{10,11},{12,13},{14,15},{16,17},{18,... | collective-permute-start | bytes 49160 | tf_op jit(solution)/shard_map/ppermute | solution.py:17
  56.6 5.4 %copy-start.13 = (bf16[2,128,128]{2,1,0:T(8,128)(2,1)S(1)}, bf16[2,128,128]{2,1,0:T(8,128)(2,1)}, u32[]{:S(2)}) copy-start(bf16[2,128,128]{2,1,0:T(8,128)(2,1)} %copy.48) | copy-start | bytes 196612
  56.6 3.6 %collective-permute-start.8 = (bf16[4,8,2,128]{3,2,1,0:T(2,128)(2,1)S(1)}, bf16[4,8,2,128]{3,2,1,0:T(2,128)(2,1)S(1)}, u32[]{:S(2)}, u32[]{:S(2)}) collective-permute-start(bf16[4,8,2,128]{3,2,1,0:T(2,128)(2,1)S(1)} %get-tuple-element.149), channel_id=1, source_target_pairs={{1,0},{3,2},{5,4},{7,6},{9,8},{11,10},{13,12},{15,14},{17,16},{19,... | collective-permute-start | bytes 49160 | tf_op jit(solution)/shard_map/ppermute | solution.py:18
  60.3 7.5 %collective-permute-start.9 = (bf16[2,8,20,128]{3,2,1,0:T(8,128)(2,1)S(1)}, bf16[2,8,20,128]{3,2,1,0:T(8,128)(2,1)S(1)}, u32[]{:S(2)}, u32[]{:S(2)}) collective-permute-start(bf16[2,8,20,128]{3,2,1,0:T(8,128)(2,1)S(1)} %pad_maximum_fusion.5), channel_id=1, source_target_pairs={{4,0},{8,4},{12,8},{5,1},{9,5},{13,9},{6,2},{10,6},{14,10},{7,3},{... | collective-permute-start | bytes 245768 | tf_op jit(solution)/shard_map/ppermute | solution.py:26
  62.0 7.0 %copy-start.11 = (bf16[5,128,128]{2,1,0:T(8,128)(2,1)S(1)}, bf16[5,128,128]{2,1,0:T(8,128)(2,1)}, u32[]{:S(2)}) copy-start(bf16[5,128,128]{2,1,0:T(8,128)(2,1)} %copy.36) | copy-start | bytes 491524
  62.3 7.0 %copy-start.10 = (bf16[5,128,128]{2,1,0:T(8,128)(2,1)S(1)}, bf16[5,128,128]{2,1,0:T(8,128)(2,1)}, u32[]{:S(2)}) copy-start(bf16[5,128,128]{2,1,0:T(8,128)(2,1)} %copy.37) | copy-start | bytes 491524
  69.0 2.8 %copy-start.1 = (bf16[4,4,16,128]{3,2,1,0:T(8,128)(2,1)S(1)}, bf16[4,4,16,128]{3,2,1,0:T(8,128)(2,1)}, u32[]{:S(2)}) copy-start(bf16[4,4,16,128]{3,2,1,0:T(8,128)(2,1)} %param.6) | copy-start | bytes 196612
  69.0 2.8 %copy-start.3 = (bf16[5,128,128]{2,1,0:T(8,128)(2,1)S(1)}, bf16[5,128,128]{2,1,0:T(8,128)(2,1)}, u32[]{:S(2)}) copy-start(bf16[5,128,128]{2,1,0:T(8,128)(2,1)} %copy.47) | copy-start | bytes 491524
  71.0 2.1 %copy-start.17 = (u32[32]{0:T(128)S(1)}, u32[32]{0:T(128)}, u32[]{:S(2)}) copy-start(u32[32]{0:T(128)} %constant.15) | copy-start | bytes 388
  (5 other events, 7.2 us)
Sparse Core Ops, SparseCore 0:
  73.2 111.9 all-reduce.3
where the time goes:
time: 196 us; the launch traced here: 195 us
  waiting for transfers between devices  82.8 us (42%)
  blocking collectives  34.5 us (18%)
  starting transfers between devices  24.6 us (13%)
  local copies, waits for them, and re-layouts  18.6 us (9%)
  between operations  15.6 us (8%)
  matrix products  12.9 us (7%)
  other arithmetic  6.33 us (3%)
    unnamed x2, waiting for transfers between devices  75.5 us
    psum x1, blocking collectives, local(): lax.psum((gamma_local, beta_local), ('gx', 'gy', 'gz'))  34.5 us
    ppermute x4, starting transfers between devices, padded_2(): before = lax.ppermute(last, axis, up)  14.3 us
    transpose x15, local copies, waits for them, and re-layouts, context_transposed(): jnp.transpose(kernel[first_tap:first_tap + count], (0, 2, 1))  9.94 us
    ppermute x2, waiting for transfers between devices, from_behind(): lax.ppermute(value, axis, [(source, source + steps) for source in range(l...  6.32 us
    unnamed x59, local copies, waits for them, and re-layouts  5.71 us
    ppermute x4, starting transfers between devices, padded_2(): after = lax.ppermute(leading, axis, down)  5.29 us
    ppermute x2, starting transfers between devices, from_behind(): lax.ppermute(value, axis, [(source, source + steps) for source in range(l...  4.96 us
  transfers between devices with their start and end apart: 11, of which 4 were waited for; matrix products, arithmetic and copies ran while one was open for 11% of the time, Pallas kernels for 0%

commit v1 on v0

--- a/solution.py
+++ b/solution.py
@@ -165,7 +165,7 @@
         preferred_element_type=jnp.float32,
     )
     beta_local = -factor * jnp.sum(weighted, axis=0)
-    grad_gamma, grad_beta = lax.psum((gamma_local, beta_local), ("gx", "gy", "gz"))
+    grad_gamma, grad_beta = lax.psum(lax.psum((gamma_local, beta_local), ("gy", "gz")), "gx")
     return (grad_features, grad_kernel, grad_gamma, grad_beta)
 
 

time: 196 us -> 263 us (1.34)
  waiting for transfers between devices: 82.8 us -> 163 us
  blocking collectives: 34.5 us -> 18.5 us
    psum x0 -> x2, waiting for transfers between devices: none -> 58.9 us  [the longest x1 34.2 us: local(): lax.psum(lax.psum((gamma_local, beta_local), ('gy', 'gz')), 'gx')]
    unnamed x2 -> x4, waiting for transfers between devices: 75.5 us -> 95.1 us
    psum x1 -> x2, blocking collectives: 34.5 us -> 18.5 us  [the longest x1 12.7 us: local(): lax.psum(lax.psum((gamma_local, beta_local), ('gy', 'gz')), 'gx')]
    unnamed x59 -> x61, local copies, waits for them, and re-layouts: 5.71 us -> 6.28 us
  transfers between devices with their start and end apart: 11 -> 13, of which waited for: 4 -> 7; matrix products, arithmetic and copies ran while one was open for 11% -> 9% of each run, Pallas kernels for 0% -> 0%
where the time goes in v1:
time: 263 us; the launch traced here: 262 us
  waiting for transfers between devices  163 us (62%)
  starting transfers between devices  24.6 us (9%)
  local copies, waits for them, and re-layouts  19 us (7%)
  blocking collectives  18.5 us (7%)
  between operations  15.3 us (6%)
  matrix products  13.1 us (5%)
  other arithmetic  8.55 us (3%)
    unnamed x4, waiting for transfers between devices  95.1 us
    psum x1, waiting for transfers between devices, local(): lax.psum(lax.psum((gamma_local, beta_local), ('gy', 'gz')), 'gx')  34.2 us
    psum x1, waiting for transfers between devices, local(): lax.psum((gamma_local, beta_local), ('gy', 'gz'))  24.7 us
    ppermute x4, starting transfers between devices, padded_2(): before = lax.ppermute(last, axis, up)  14.3 us
    psum x1, blocking collectives, local(): lax.psum(lax.psum((gamma_local, beta_local), ('gy', 'gz')), 'gx')  12.7 us
    transpose x15, local copies, waits for them, and re-layouts, context_transposed(): jnp.transpose(kernel[first_tap:first_tap + count], (0, 2, 1))  9.84 us
    unnamed x61, local copies, waits for them, and re-layouts  6.28 us
    ppermute x2, waiting for transfers between devices, from_behind(): lax.ppermute(value, axis, [(source, source + steps) for source in range(l...  6.21 us
  transfers between devices with their start and end apart: 13, of which 7 were waited for; matrix products, arithmetic and copies ran while one was open for 9% of the time, Pallas kernels for 0%

profile of v1, /device:TPU:0, one launch (start us, length us, event | category | flops | bytes accessed | tf_op | source)
XLA Modules:
  0.0 261.9 jit_solution(14108300536108189736)
XLA Ops:
  8.1 1.2 fusion.12
  9.3 4.9 %collective-permute-start = (bf16[4,2,16,128]{3,2,1,0:T(8,128)(2,1)S(1)}, bf16[4,2,16,128]{3,2,1,0:T(8,128)(2,1)S(1)}, u32[]{:S(2)}, u32[]{:S(2)}) collective-permute-start(bf16[4,2,16,128]{3,2,1,0:T(8,128)(2,1)S(1)} %get-tuple-element.158), channel_id=1, source_target_pairs={{0,2},{1,3},{4,6},{5,7},{8,10},{9,11},{12,14},{13,15},{16,18},{17,... | collective-permute-start | bytes 98312 | tf_op jit(solution)/shard_map/ppermute | solution.py:17
  14.2 1.3 collective-permute-start.1
  15.5 2.2 fusion.16
  17.7 2.9 %slice_bitcast_fusion.1 = (bf16[5,128,128]{1,2,0:T(8,128)(2,1)S(1)}, bf16[5,128,128]{1,2,0:T(8,128)(2,1)S(1)}, bf16[5,128,128]{1,2,0:T(8,128)(2,1)S(1)}, bf16[5,...) fusion(bf16[62,128,128]{2,1,0:T(8,128)(2,1)} %param.9), kind=kLoop, calls=%fused_computation.212 | loop fusion | bytes 5079040 | tf_op jit(solution)/shard_map/transpose | solution.py:94
  22.1 1.3 collective-permute-start.3
  23.4 3.6 %collective-permute-start.2 = (bf16[4,8,2,128]{3,2,1,0:T(2,128)(2,1)}, bf16[4,8,2,128]{3,2,1,0:T(2,128)(2,1)}, u32[]{:S(2)}, u32[]{:S(2)}) collective-permute-start(bf16[4,8,2,128]{3,2,1,0:T(2,128)(2,1)} %get-tuple-element.151), channel_id=1, source_target_pairs={{0,1},{2,3},{4,5},{6,7},{8,9},{10,11},{12,13},{14,15},{16,17},{18,... | collective-permute-start | bytes 49160 | tf_op jit(solution)/shard_map/ppermute | solution.py:17
  33.9 3.5 %collective-permute-start.4 = (bf16[2,8,20,128]{3,2,1,0:T(8,128)(2,1)S(1)}, bf16[2,8,20,128]{3,2,1,0:T(8,128)(2,1)S(1)}, u32[]{:S(2)}, u32[]{:S(2)}) collective-permute-start(bf16[2,8,20,128]{3,2,1,0:T(8,128)(2,1)S(1)} %pad_maximum_fusion.9), channel_id=1, source_target_pairs={{0,4},{4,8},{8,12},{1,5},{5,9},{9,13},{2,6},{6,10},{10,14},{3,7},{... | collective-permute-start | bytes 245768 | tf_op jit(solution)/shard_map/ppermute | solution.py:26
  44.9 4.5 %collective-permute-start.5 = (bf16[4,2,16,128]{3,2,1,0:T(8,128)(2,1)S(1)}, bf16[4,2,16,128]{3,2,1,0:T(8,128)(2,1)S(1)}, u32[]{:S(2)}, u32[]{:S(2)}) collective-permute-start(bf16[4,2,16,128]{3,2,1,0:T(8,128)(2,1)S(1)} %get-tuple-element.156), channel_id=1, source_target_pairs={{0,2},{1,3},{4,6},{5,7},{8,10},{9,11},{12,14},{13,15},{16,18},{17,... | collective-permute-start | bytes 98312 | tf_op jit(solution)/shard_map/ppermute | solution.py:17
  49.5 1.3 collective-permute-start.6
  54.1 1.2 collective-permute-done.6
  55.3 1.3 collective-permute-start.7
  56.6 1.3 collective-permute-start.8
  58.2 1.5 collective-permute-done.8
  59.8 1.5 collective-permute-start.9
  61.9 5.3 %collective-permute-done.9 = bf16[2,8,20,128]{3,2,1,0:T(8,128)(2,1)S(1)} collective-permute-done((bf16[2,8,20,128]{3,2,1,0:T(8,128)(2,1)S(1)}, bf16[2,8,20,128]{3,2,1,0:T(8,128)(2,1)S(1)}, u32[]{:S(2)}, u32[]{:S(2)}) %collective-permute-start.9) | collective-permute-done | bytes 81952 | tf_op jit(solution)/shard_map/ppermute | solution.py:26
  72.6 4.4 %multiply_bitcast_fusion = f32[1015808]{0:T(1024)} fusion(f32[7936,128]{1,0:T(8,128)} %copy-done.1), kind=kLoop, calls=%fused_computation | loop fusion | flops 1015808 | bytes 8126464 | tf_op jit(solution)/shard_map/div | solution.py:156
  79.8 24.7 %all-reduce.5.cloned.1.call-done = f32[128,128]{1,0:T(8,128)} async-done(((f32[128,128]{1,0:T(8,128)}), f32[128,128]{1,0:T(8,128)}) %all-reduce.5.cloned.1.call-update) | async-done | bytes 65552 | tf_op jit(solution)/shard_map/psum | solution.py:168
  104.6 5.8 %psum.30 = f32[128]{0:T(128)S(1)} all-reduce(f32[128]{0:T(128)S(1)} %broadcast_multiply_fusion), channel_id=1, replica_groups=mesh['groups'=2,'gx'=4,'gy'=2,'gz'=2] {'gy','gz'}, use_global_device_ids=true, to_apply=%region_4.0 | all-reduce | flops 128 | bytes 1024 | tf_op jit(solution)/shard_map/psum | solution.py:168
  110.4 12.7 %psum.31 = f32[128]{0:T(128)} all-reduce(f32[128]{0:T(128)S(1)} %psum.30), channel_id=1, replica_groups=mesh['groups'=2,'gx'=4,'gy'=2,'gz'=2] {'gx'}, use_global_device_ids=true, to_apply=%region_5.0 | all-reduce | flops 128 | bytes 1024 | tf_op jit(solution)/shard_map/psum | solution.py:168
  123.1 95.0 %all-reduce.9.cloned.1.call-done = f32[1015808]{0:T(1024)} async-done(((f32[1015808]{0:T(1024)}), f32[1015808]{0:T(1024)}) %all-reduce.9.cloned.1.call-update) | async-done | bytes 4063248
  218.1 1.7 dynamic-slice.1
  219.8 34.2 %all-reduce.7.cloned.1.call-done = f32[128,128]{1,0:T(8,128)} async-done(((f32[128,128]{1,0:T(8,128)}), f32[128,128]{1,0:T(8,128)}) %all-reduce.7.cloned.1.call-update) | async-done | bytes 65552 | tf_op jit(solution)/shard_map/psum | solution.py:168
  253.9 1.5 copy.160
  (152 shorter events, 27.9 us)
Async XLA Ops:
  7.2 97.4 %all-reduce.5.cloned.1.call-start = ((), (), s32[]{:S(2)}) async-start(), calls=%async_computation | async-start | bytes 131072 | tf_op jit(solution)/shard_map/psum | solution.py:168
  8.1 18.9 %copy-start.15 = (bf16[4,4,16,128]{3,2,1,0:T(8,128)(2,1)S(1)}, bf16[4,4,16,128]{3,2,1,0:T(8,128)(2,1)}, u32[]{:S(2)}) copy-start(bf16[4,4,16,128]{3,2,1,0:T(8,128)(2,1)} %param.7) | copy-start | bytes 196612
  9.3 12.1 %collective-permute-start = (bf16[4,2,16,128]{3,2,1,0:T(8,128)(2,1)S(1)}, bf16[4,2,16,128]{3,2,1,0:T(8,128)(2,1)S(1)}, u32[]{:S(2)}, u32[]{:S(2)}) collective-permute-start(bf16[4,2,16,128]{3,2,1,0:T(8,128)(2,1)S(1)} %get-tuple-element.158), channel_id=1, source_target_pairs={{0,2},{1,3},{4,6},{5,7},{8,10},{9,11},{12,14},{13,15},{16,18},{17,... | collective-permute-start | bytes 98312 | tf_op jit(solution)/shard_map/ppermute | solution.py:17
  14.2 7.2 %collective-permute-start.1 = (bf16[4,2,16,128]{3,2,1,0:T(8,128)(2,1)S(1)}, bf16[4,2,16,128]{3,2,1,0:T(8,128)(2,1)S(1)}, u32[]{:S(2)}, u32[]{:S(2)}) collective-permute-start(bf16[4,2,16,128]{3,2,1,0:T(8,128)(2,1)S(1)} %get-tuple-element.159), channel_id=1, source_target_pairs={{2,0},{3,1},{6,4},{7,5},{10,8},{11,9},{14,12},{15,13},{18,16},{19,... | collective-permute-start | bytes 98312 | tf_op jit(solution)/shard_map/ppermute | solution.py:18
  22.1 11.0 %collective-permute-start.3 = (bf16[4,8,2,128]{3,2,1,0:T(2,128)(2,1)}, bf16[4,8,2,128]{3,2,1,0:T(2,128)(2,1)S(1)}, u32[]{:S(2)}, u32[]{:S(2)}) collective-permute-start(bf16[4,8,2,128]{3,2,1,0:T(2,128)(2,1)} %get-tuple-element.150), channel_id=1, source_target_pairs={{1,0},{3,2},{5,4},{7,6},{9,8},{11,10},{13,12},{15,14},{17,16},{19,... | collective-permute-start | bytes 49160 | tf_op jit(solution)/shard_map/ppermute | solution.py:18
  23.4 9.7 %collective-permute-start.2 = (bf16[4,8,2,128]{3,2,1,0:T(2,128)(2,1)}, bf16[4,8,2,128]{3,2,1,0:T(2,128)(2,1)}, u32[]{:S(2)}, u32[]{:S(2)}) collective-permute-start(bf16[4,8,2,128]{3,2,1,0:T(2,128)(2,1)} %get-tuple-element.151), channel_id=1, source_target_pairs={{0,1},{2,3},{4,5},{6,7},{8,9},{10,11},{12,13},{14,15},{16,17},{18,... | collective-permute-start | bytes 49160 | tf_op jit(solution)/shard_map/ppermute | solution.py:17
  33.9 5.7 %collective-permute-start.4 = (bf16[2,8,20,128]{3,2,1,0:T(8,128)(2,1)S(1)}, bf16[2,8,20,128]{3,2,1,0:T(8,128)(2,1)S(1)}, u32[]{:S(2)}, u32[]{:S(2)}) collective-permute-start(bf16[2,8,20,128]{3,2,1,0:T(8,128)(2,1)S(1)} %pad_maximum_fusion.9), channel_id=1, source_target_pairs={{0,4},{4,8},{8,12},{1,5},{5,9},{9,13},{2,6},{6,10},{10,14},{3,7},{... | collective-permute-start | bytes 245768 | tf_op jit(solution)/shard_map/ppermute | solution.py:26
  38.3 3.2 %copy-start.8 = (bf16[5,128,128]{2,1,0:T(8,128)(2,1)S(1)}, bf16[5,128,128]{2,1,0:T(8,128)(2,1)}, u32[]{:S(2)}) copy-start(bf16[5,128,128]{2,1,0:T(8,128)(2,1)} %get-tuple-element.31) | copy-start | bytes 491524
  38.6 3.2 %copy-start.7 = (bf16[5,128,128]{2,1,0:T(8,128)(2,1)S(1)}, bf16[5,128,128]{2,1,0:T(8,128)(2,1)}, u32[]{:S(2)}) copy-start(bf16[5,128,128]{2,1,0:T(8,128)(2,1)} %get-tuple-element.30) | copy-start | bytes 491524
  41.5 2.8 %copy-start.13 = (bf16[5,128,128]{2,1,0:T(8,128)(2,1)S(1)}, bf16[5,128,128]{2,1,0:T(8,128)(2,1)}, u32[]{:S(2)}) copy-start(bf16[5,128,128]{2,1,0:T(8,128)(2,1)} %get-tuple-element.27) | copy-start | bytes 491524
  41.5 2.8 %copy-start.17 = (f32[256]{0:T(256)S(1)}, f32[256]{0:T(256)}, u32[]{:S(2)}) copy-start(f32[256]{0:T(256)} %copy-done.16) | copy-start | bytes 3076
  44.9 9.2 %collective-permute-start.5 = (bf16[4,2,16,128]{3,2,1,0:T(8,128)(2,1)S(1)}, bf16[4,2,16,128]{3,2,1,0:T(8,128)(2,1)S(1)}, u32[]{:S(2)}, u32[]{:S(2)}) collective-permute-start(bf16[4,2,16,128]{3,2,1,0:T(8,128)(2,1)S(1)} %get-tuple-element.156), channel_id=1, source_target_pairs={{0,2},{1,3},{4,6},{5,7},{8,10},{9,11},{12,14},{13,15},{16,18},{17,... | collective-permute-start | bytes 98312 | tf_op jit(solution)/shard_map/ppermute | solution.py:17
  49.5 5.8 %collective-permute-start.6 = (bf16[4,2,16,128]{3,2,1,0:T(8,128)(2,1)S(1)}, bf16[4,2,16,128]{3,2,1,0:T(8,128)(2,1)S(1)}, u32[]{:S(2)}, u32[]{:S(2)}) collective-permute-start(bf16[4,2,16,128]{3,2,1,0:T(8,128)(2,1)S(1)} %get-tuple-element.157), channel_id=1, source_target_pairs={{2,0},{3,1},{6,4},{7,5},{10,8},{11,9},{14,12},{15,13},{18,16},{19,... | collective-permute-start | bytes 98312 | tf_op jit(solution)/shard_map/ppermute | solution.py:18
  51.7 9.8 %copy-start.14 = (bf16[2,128,128]{2,1,0:T(8,128)(2,1)S(1)}, bf16[2,128,128]{2,1,0:T(8,128)(2,1)}, u32[]{:S(2)}) copy-start(bf16[2,128,128]{2,1,0:T(8,128)(2,1)} %copy.48) | copy-start | bytes 196612
  55.3 2.8 %collective-permute-start.7 = (bf16[4,8,2,128]{3,2,1,0:T(2,128)(2,1)S(1)}, bf16[4,8,2,128]{3,2,1,0:T(2,128)(2,1)S(1)}, u32[]{:S(2)}, u32[]{:S(2)}) collective-permute-start(bf16[4,8,2,128]{3,2,1,0:T(2,128)(2,1)S(1)} %get-tuple-element.146), channel_id=1, source_target_pairs={{0,1},{2,3},{4,5},{6,7},{8,9},{10,11},{12,13},{14,15},{16,17},{18,... | collective-permute-start | bytes 49160 | tf_op jit(solution)/shard_map/ppermute | solution.py:17
  56.6 3.1 %collective-permute-start.8 = (bf16[4,8,2,128]{3,2,1,0:T(2,128)(2,1)S(1)}, bf16[4,8,2,128]{3,2,1,0:T(2,128)(2,1)S(1)}, u32[]{:S(2)}, u32[]{:S(2)}) collective-permute-start(bf16[4,8,2,128]{3,2,1,0:T(2,128)(2,1)S(1)} %get-tuple-element.147), channel_id=1, source_target_pairs={{1,0},{3,2},{5,4},{7,6},{9,8},{11,10},{13,12},{15,14},{17,16},{19,... | collective-permute-start | bytes 49160 | tf_op jit(solution)/shard_map/ppermute | solution.py:18
  58.2 3.7 %copy-start.1 = (f32[7936,128]{1,0:T(8,128)}, f32[7936,128]{1,0:T(8,128)S(1)}, u32[]{:S(2)}) copy-start(f32[7936,128]{1,0:T(8,128)S(1)} %convolution_dynamic-update-slice_fusion.12) | copy-start | bytes 12189700
  59.8 7.4 %collective-permute-start.9 = (bf16[2,8,20,128]{3,2,1,0:T(8,128)(2,1)S(1)}, bf16[2,8,20,128]{3,2,1,0:T(8,128)(2,1)S(1)}, u32[]{:S(2)}, u32[]{:S(2)}) collective-permute-start(bf16[2,8,20,128]{3,2,1,0:T(8,128)(2,1)S(1)} %pad_maximum_fusion.5), channel_id=1, source_target_pairs={{4,0},{8,4},{12,8},{5,1},{9,5},{13,9},{6,2},{10,6},{14,10},{7,3},{... | collective-permute-start | bytes 245768 | tf_op jit(solution)/shard_map/ppermute | solution.py:26
  61.5 6.9 %copy-start.12 = (bf16[5,128,128]{2,1,0:T(8,128)(2,1)S(1)}, bf16[5,128,128]{2,1,0:T(8,128)(2,1)}, u32[]{:S(2)}) copy-start(bf16[5,128,128]{2,1,0:T(8,128)(2,1)} %copy.36) | copy-start | bytes 491524
  61.8 6.9 %copy-start.11 = (bf16[5,128,128]{2,1,0:T(8,128)(2,1)S(1)}, bf16[5,128,128]{2,1,0:T(8,128)(2,1)}, u32[]{:S(2)}) copy-start(bf16[5,128,128]{2,1,0:T(8,128)(2,1)} %copy.37) | copy-start | bytes 491524
  68.4 2.8 %copy-start.2 = (bf16[4,4,16,128]{3,2,1,0:T(8,128)(2,1)S(1)}, bf16[4,4,16,128]{3,2,1,0:T(8,128)(2,1)}, u32[]{:S(2)}) copy-start(bf16[4,4,16,128]{3,2,1,0:T(8,128)(2,1)} %param.6) | copy-start | bytes 196612
  68.4 2.8 %copy-start.4 = (bf16[5,128,128]{2,1,0:T(8,128)(2,1)S(1)}, bf16[5,128,128]{2,1,0:T(8,128)(2,1)}, u32[]{:S(2)}) copy-start(bf16[5,128,128]{2,1,0:T(8,128)(2,1)} %copy.47) | copy-start | bytes 491524
  72.6 145.6 %all-reduce.9.cloned.1.call-start = ((), (), s32[]{:S(2)}) async-start(), calls=%async_computation.2 | async-start | bytes 8126464
  77.1 176.9 %all-reduce.7.cloned.1.call-start = ((), (), s32[]{:S(2)}) async-start(), calls=%async_computation.1 | async-start | bytes 131072 | tf_op jit(solution)/shard_map/psum | solution.py:168
  (8 other events, 11.7 us)
Sparse Core Ops, SparseCore 0:
  72.7 31.8 all-reduce.4
  108.2 109.8 all-reduce.8
  220.5 33.4 all-reduce.6
